TPU v7x, 32 devices: a whole 2x2x4 slice. The times are simulated.
32 devices in a mesh: users: 16 (over z, y, x), rep: 2 (over core).
Axes of the slice: x: 2, y: 2, z: 4, core: 2. Of those that a mesh axis runs over, the one named last changes fastest.
Arguments:
- user_factors: float32 [16384, 256], P('users'), may hold values from -1.5 to 1.5
- user_accum: float32 [16384, 256], P('users'), may hold values from 0.5 to 8
- item_factors: float32 [4096, 256], P('users'), may hold values from -1.5 to 1.5
- item_accum: float32 [4096, 256], P('users'), may hold values from 0.5 to 8
- tile_counts: bfloat16 [16, 2, 128, 128, 128], P('users', 'rep'), may hold values from 0 to 20, as said below
- tile_user: int32 [16, 2, 128], P('users', 'rep'), may hold values from 0 to 7
- tile_item: int32 [16, 2, 128], P('users', 'rep'), may hold values from 0 to 31, as said below
- send_list: int32 [16, 2, 16], P('users', 'rep'), may hold values from 0 to 2, as said below
Outputs:
- new_users: float32 [16384, 256], P('users')
- new_user_accum: float32 [16384, 256], P('users')
- new_items: float32 [4096, 256], P('users')
- new_item_accum: float32 [4096, 256], P('users')
Inputs may be any that keep to these rules, and one draw needn't show every extreme that they name: `tile_counts`: zero means no interaction. `tile_item`: panel b belongs to owner b // 2. Device (q, r) uses at most one panel of each owner o, namely o * 2 + send_list[o, r, q], and only where send_list[o, r, q] < 2. `send_list`: the value 2 means that requester q uses no panel of owner o.
All inputs are finite; a program needn't handle non-finite values.
Results may differ from a plain program's by a relative error of at most 0.0026.
Values may be sent and summed in bfloat16 or wider, within the bound.
No kernel may reach another device: no remote copies, remote signals or barrier semaphores. Data moves between devices by JAX's collectives and lax.ppermute only.
A program may use at most 128 MiB of HBM per device.

v0:
```python
import math
import jax
import jax.numpy as jnp
from jax import lax
from jax.sharding import PartitionSpec as P

CONF_SLOPE = 0.5
ERR_SCALE = 1.0 / 64.0


def tile_terms(user_strip, panels, counts, users_idx, fetch_index, slot_index, slot_count):
    tile_count = counts.shape[0]
    group_size = math.gcd(tile_count, 32)
    group_count = tile_count // group_size
    side = counts.shape[-1]
    width = panels.shape[-1]

    def tile_step(totals, inputs):
        user_total, slot_total = totals
        block_counts, block_user, block_fetch, block_slot = inputs
        user_rows = user_strip[block_user]
        item_rows = panels[block_fetch]
        predicted = jnp.einsum(
            "gur,gir->gui", user_rows, item_rows, preferred_element_type=jnp.float32
        )
        amount = block_counts.astype(jnp.float32)
        confidence = 1.0 + CONF_SLOPE * amount
        preference = jnp.where(amount > 0, 1.0, 0.0).astype(jnp.float32)
        weighted_err = (confidence * (predicted - preference) * ERR_SCALE).astype(jnp.bfloat16)
        user_part = jnp.einsum(
            "gui,gir->gur", weighted_err, item_rows, preferred_element_type=jnp.float32
        )
        item_part = jnp.einsum(
            "gui,gur->gir", weighted_err, user_rows, preferred_element_type=jnp.float32
        )
        user_total = user_total.at[block_user].add(user_part)
        slot_total = slot_total.at[block_slot].add(item_part)
        return ((user_total, slot_total), None)

    start = (
        jnp.zeros((user_strip.shape[0], side, width), jnp.float32),
        jnp.zeros((slot_count, side, width), jnp.float32),
    )
    inputs = (
        counts.reshape(group_count, group_size, side, side),
        users_idx.reshape(group_count, group_size),
        fetch_index.reshape(group_count, group_size),
        slot_index.reshape(group_count, group_size),
    )
    (user_total, slot_total), _ = lax.scan(tile_step, start, inputs)
    return (user_total, slot_total)


def adagrad(factors, accum, grad):
    new_accum = accum + grad * grad
    return (factors - grad / jnp.sqrt(new_accum), new_accum)


def local(
    user_factors, user_accum, item_factors, item_accum, tile_counts, tile_user, tile_item, send_list
):
    tile_size = tile_counts.shape[-1]
    feat_width = user_factors.shape[1]
    user_strip = user_factors.astype(jnp.bfloat16).reshape(-1, tile_size, feat_width)
    owned_panels = item_factors.astype(jnp.bfloat16).reshape(-1, tile_size, feat_width)
    panels_own = owned_panels.shape[0]
    peer_count = lax.axis_size("users")
    counts = tile_counts[0, 0]
    users_idx = tile_user[0, 0]
    items_idx = tile_item[0, 0]
    send_row = send_list[0, 0]
    slot_index = items_idx // panels_own
    outgoing = owned_panels[jnp.minimum(send_row, panels_own - 1)]
    panels = lax.all_to_all(outgoing, "users", split_axis=0, concat_axis=0, tiled=True)
    user_part, slot_part = tile_terms(
        user_strip, panels, counts, users_idx, slot_index, slot_index, peer_count
    )
    returned = lax.all_to_all(
        slot_part.astype(jnp.bfloat16), "users", split_axis=0, concat_axis=0, tiled=True
    )
    selector = (send_row[None, :] == jnp.arange(panels_own, dtype=jnp.int32)[:, None]).astype(
        jnp.bfloat16
    )
    item_part = jnp.einsum("kq,qir->kir", selector, returned, preferred_element_type=jnp.float32)
    item_part = item_part.reshape(-1, feat_width)
    user_grad = lax.psum(user_part.reshape(-1, feat_width), "rep")
    new_users, new_user_accum = adagrad(user_factors, user_accum, user_grad)
    item_grad = lax.psum(item_part, "rep")
    new_items, new_item_accum = adagrad(item_factors, item_accum, item_grad)
    return (new_users, new_user_accum, new_items, new_item_accum)


def solution(mesh):
    return jax.shard_map(
        local,
        mesh=mesh,
        in_specs=(
            P("users", None),
            P("users", None),
            P("users", None),
            P("users", None),
            P("users", "rep", None, None, None),
            P("users", "rep", None),
            P("users", "rep", None),
            P("users", "rep", None),
        ),
        out_specs=(P("users", None), P("users", None), P("users", None), P("users", None)),
        check_vma=False,
    )
```

profile of v0, /device:TPU:0, one launch (start us, length us, event | category | flops | bytes accessed | tf_op | source)
XLA Modules:
  0.0 230.2 jit_solution(15211641022157744401)
XLA Ops:
  7.2 0.7 fusion.16
  7.8 1.0 convert_element_type.20
  8.8 1.6 gather_fusion.2
  10.4 8.3 %all-to-all-start = ((bf16[16,128,256]{2,1,0:T(8,128)(2,1)}), bf16[16,128,256]{2,1,0:T(8,128)(2,1)S(1)}, u32[]{:S(2)}, u32[]{:S(2)}) async-start(bf16[16,128,256]{2,1,0:T(8,128)(2,1)} %gather_fusion.2), calls=%async_computation | async-start | bytes 2097152 | tf_op jit(solution)/shard_map/all_to_all | solution.py:74
  19.3 0.7 reduce.6
  20.0 0.7 reduce.7
  20.8 0.9 convert_element_type.19
  21.7 21.4 %all-to-all-done = bf16[16,128,256]{2,1,0:T(8,128)(2,1)S(1)} async-done(((bf16[16,128,256]{2,1,0:T(8,128)(2,1)}), bf16[16,128,256]{2,1,0:T(8,128)(2,1)S(1)}, u32[]{:S(2)}, u32[]{:S(2)}) %all-to-all-start) | async-done | bytes 1048608 | tf_op jit(solution)/shard_map/all_to_all | solution.py:74
  43.2 1.0 copy-done.2
  44.4 123.8 %while.13 = (s32[]{:T(128)}, f32[8,128,256]{2,1,0:T(8,128)S(1)}, f32[16,128,256]{2,1,0:T(8,128)S(1)}, s32[4,32]{1,0:T(4,128)S(1)}, bf16[4,32,128,128]{3,2,1,0:T(...) while((s32[]{:T(128)}, f32[8,128,256]{2,1,0:T(8,128)S(1)}, ...), condition=%wide.region_3.4_spmd, body=%wide.region_0.3_spmd.sunk | while | flops 812124352 | bytes 67118496 | solution.py:50
  44.5 3.2 %gather_fusion.1 = bf16[32,128,256]{2,1,0:T(8,128)(2,1)} fusion(bf16[16,128,256]{2,1,0:T(8,128)(2,1)} %get-tuple-element.173, s32[1024]{0:T(1024)S(1)} %pad_clamp_fusion.6), kind=kCustom, calls=%fused_computation.1.clone.1 | custom fusion | bytes 4194432 | tf_op jit(solution)/shard_map/while/body/eval_jaxpr/gather | solution.py:22
  47.7 3.1 %gather_fusion = bf16[32,128,256]{2,1,0:T(8,128)(2,1)} fusion(bf16[8,128,256]{2,1,0:T(8,128)(2,1)} %get-tuple-element.171, s32[1024]{0:T(1024)S(1)} %pad_clamp_fusion.5), kind=kCustom, calls=%fused_computation.clone.1 | custom fusion | bytes 4194432 | tf_op jit(solution)/shard_map/while/body/eval_jaxpr/gather | solution.py:21
  50.8 3.4 %fusion.43 = bf16[32,128,128]{2,1,0:T(8,128)(2,1)S(1)} fusion(bf16[32,128,256]{2,1,0:T(8,128)(2,1)} %gather_fusion, bf16[32,128,256]{2,1,0:T(8,128)(2,1)} %gather_fusion.1, bf16[4,32,128,128]{3,2,1,0:T(8,128)(2,1)} %get-tuple-element.170, s32[]{:T(128)S(6)} %copy.28), kind=kOutput, calls=%fused_computation.11.clone.1 | convolution fusion | flops 273154048 | bytes 6291460 | tf_op jit(solution)/shard_map/while/body/eval_jaxpr/gur,gir->gui/dot_general | solution.py:23
  54.2 1.0 copy-done.3
  55.2 2.7 %fusion.45 = f32[32,128,256]{2,1,0:T(8,128)} fusion(bf16[32,128,128]{2,1,0:T(8,128)(2,1)S(1)} %fusion.43, bf16[32,128,256]{2,1,0:T(8,128)(2,1)S(1)} %copy-done.1), kind=kOutput, calls=%fused_computation.44.clone.1 | convolution fusion | flops 268435456 | bytes 7340032 | tf_op jit(solution)/shard_map/while/body/eval_jaxpr/gui,gur->gir/dot_general | solution.py:33
  57.9 6.5 %scatter_fusion.1 = f32[16,128,256]{2,1,0:T(8,128)S(1)} fusion(f32[16,128,256]{2,1,0:T(8,128)S(1)} %get-tuple-element.159, s32[32]{0:T(128)S(1)} %get-tuple-element.147, f32[32,128,256]{2,1,0:T(8,128)} %fusion.45), kind=kCustom, calls=%fused_computation.4.clone.1 | custom fusion | flops 1048576 | bytes 12583040 | tf_op jit(solution)/shard_map/while/body/eval_jaxpr/scatter-add | solution.py:37
  64.3 4.6 %fusion.44 = f32[32,128,256]{2,1,0:T(8,128)} fusion(bf16[32,128,128]{2,1,0:T(8,128)(2,1)} %copy-done.3, bf16[32,128,256]{2,1,0:T(8,128)(2,1)} %gather_fusion.1), kind=kOutput, calls=%fused_computation.43.clone.1 | convolution fusion | flops 268435456 | bytes 7340032 | tf_op jit(solution)/shard_map/while/body/eval_jaxpr/gui,gir->gur/dot_general | solution.py:30
  68.9 6.5 %scatter_fusion = f32[8,128,256]{2,1,0:T(8,128)S(1)} fusion(f32[8,128,256]{2,1,0:T(8,128)S(1)} %get-tuple-element.158, s32[32]{0:T(128)S(1)} %get-tuple-element.146, f32[32,128,256]{2,1,0:T(8,128)} %fusion.44), kind=kCustom, calls=%fused_computation.3.clone.1 | custom fusion | flops 1048576 | bytes 12583040 | tf_op jit(solution)/shard_map/while/body/eval_jaxpr/scatter-add | solution.py:36
  75.4 3.2 %gather_fusion.1 = bf16[32,128,256]{2,1,0:T(8,128)(2,1)} fusion(bf16[16,128,256]{2,1,0:T(8,128)(2,1)} %get-tuple-element.173, s32[1024]{0:T(1024)S(1)} %pad_clamp_fusion.6), kind=kCustom, calls=%fused_computation.1.clone.1 | custom fusion | bytes 4194432 | tf_op jit(solution)/shard_map/while/body/eval_jaxpr/gather | solution.py:22
  78.7 3.1 %gather_fusion = bf16[32,128,256]{2,1,0:T(8,128)(2,1)} fusion(bf16[8,128,256]{2,1,0:T(8,128)(2,1)} %get-tuple-element.171, s32[1024]{0:T(1024)S(1)} %pad_clamp_fusion.5), kind=kCustom, calls=%fused_computation.clone.1 | custom fusion | bytes 4194432 | tf_op jit(solution)/shard_map/while/body/eval_jaxpr/gather | solution.py:21
  81.7 3.4 %fusion.43 = bf16[32,128,128]{2,1,0:T(8,128)(2,1)S(1)} fusion(bf16[32,128,256]{2,1,0:T(8,128)(2,1)} %gather_fusion, bf16[32,128,256]{2,1,0:T(8,128)(2,1)} %gather_fusion.1, bf16[4,32,128,128]{3,2,1,0:T(8,128)(2,1)} %get-tuple-element.170, s32[]{:T(128)S(6)} %copy.28), kind=kOutput, calls=%fused_computation.11.clone.1 | convolution fusion | flops 273154048 | bytes 6291460 | tf_op jit(solution)/shard_map/while/body/eval_jaxpr/gur,gir->gui/dot_general | solution.py:23
  85.1 1.0 copy-done.3
  86.1 2.7 %fusion.45 = f32[32,128,256]{2,1,0:T(8,128)} fusion(bf16[32,128,128]{2,1,0:T(8,128)(2,1)S(1)} %fusion.43, bf16[32,128,256]{2,1,0:T(8,128)(2,1)S(1)} %copy-done.1), kind=kOutput, calls=%fused_computation.44.clone.1 | convolution fusion | flops 268435456 | bytes 7340032 | tf_op jit(solution)/shard_map/while/body/eval_jaxpr/gui,gur->gir/dot_general | solution.py:33
  88.8 6.5 %scatter_fusion.1 = f32[16,128,256]{2,1,0:T(8,128)S(1)} fusion(f32[16,128,256]{2,1,0:T(8,128)S(1)} %get-tuple-element.159, s32[32]{0:T(128)S(1)} %get-tuple-element.147, f32[32,128,256]{2,1,0:T(8,128)} %fusion.45), kind=kCustom, calls=%fused_computation.4.clone.1 | custom fusion | flops 1048576 | bytes 12583040 | tf_op jit(solution)/shard_map/while/body/eval_jaxpr/scatter-add | solution.py:37
  95.3 4.6 %fusion.44 = f32[32,128,256]{2,1,0:T(8,128)} fusion(bf16[32,128,128]{2,1,0:T(8,128)(2,1)} %copy-done.3, bf16[32,128,256]{2,1,0:T(8,128)(2,1)} %gather_fusion.1), kind=kOutput, calls=%fused_computation.43.clone.1 | convolution fusion | flops 268435456 | bytes 7340032 | tf_op jit(solution)/shard_map/while/body/eval_jaxpr/gui,gir->gur/dot_general | solution.py:30
  99.8 6.5 %scatter_fusion = f32[8,128,256]{2,1,0:T(8,128)S(1)} fusion(f32[8,128,256]{2,1,0:T(8,128)S(1)} %get-tuple-element.158, s32[32]{0:T(128)S(1)} %get-tuple-element.146, f32[32,128,256]{2,1,0:T(8,128)} %fusion.44), kind=kCustom, calls=%fused_computation.3.clone.1 | custom fusion | flops 1048576 | bytes 12583040 | tf_op jit(solution)/shard_map/while/body/eval_jaxpr/scatter-add | solution.py:36
  106.4 3.2 %gather_fusion.1 = bf16[32,128,256]{2,1,0:T(8,128)(2,1)} fusion(bf16[16,128,256]{2,1,0:T(8,128)(2,1)} %get-tuple-element.173, s32[1024]{0:T(1024)S(1)} %pad_clamp_fusion.6), kind=kCustom, calls=%fused_computation.1.clone.1 | custom fusion | bytes 4194432 | tf_op jit(solution)/shard_map/while/body/eval_jaxpr/gather | solution.py:22
  109.6 3.1 %gather_fusion = bf16[32,128,256]{2,1,0:T(8,128)(2,1)} fusion(bf16[8,128,256]{2,1,0:T(8,128)(2,1)} %get-tuple-element.171, s32[1024]{0:T(1024)S(1)} %pad_clamp_fusion.5), kind=kCustom, calls=%fused_computation.clone.1 | custom fusion | bytes 4194432 | tf_op jit(solution)/shard_map/while/body/eval_jaxpr/gather | solution.py:21
  112.7 3.4 %fusion.43 = bf16[32,128,128]{2,1,0:T(8,128)(2,1)S(1)} fusion(bf16[32,128,256]{2,1,0:T(8,128)(2,1)} %gather_fusion, bf16[32,128,256]{2,1,0:T(8,128)(2,1)} %gather_fusion.1, bf16[4,32,128,128]{3,2,1,0:T(8,128)(2,1)} %get-tuple-element.170, s32[]{:T(128)S(6)} %copy.28), kind=kOutput, calls=%fused_computation.11.clone.1 | convolution fusion | flops 273154048 | bytes 6291460 | tf_op jit(solution)/shard_map/while/body/eval_jaxpr/gur,gir->gui/dot_general | solution.py:23
  116.1 1.0 copy-done.3
  117.0 2.7 %fusion.45 = f32[32,128,256]{2,1,0:T(8,128)} fusion(bf16[32,128,128]{2,1,0:T(8,128)(2,1)S(1)} %fusion.43, bf16[32,128,256]{2,1,0:T(8,128)(2,1)S(1)} %copy-done.1), kind=kOutput, calls=%fused_computation.44.clone.1 | convolution fusion | flops 268435456 | bytes 7340032 | tf_op jit(solution)/shard_map/while/body/eval_jaxpr/gui,gur->gir/dot_general | solution.py:33
  119.7 6.5 %scatter_fusion.1 = f32[16,128,256]{2,1,0:T(8,128)S(1)} fusion(f32[16,128,256]{2,1,0:T(8,128)S(1)} %get-tuple-element.159, s32[32]{0:T(128)S(1)} %get-tuple-element.147, f32[32,128,256]{2,1,0:T(8,128)} %fusion.45), kind=kCustom, calls=%fused_computation.4.clone.1 | custom fusion | flops 1048576 | bytes 12583040 | tf_op jit(solution)/shard_map/while/body/eval_jaxpr/scatter-add | solution.py:37
  126.2 4.5 %fusion.44 = f32[32,128,256]{2,1,0:T(8,128)} fusion(bf16[32,128,128]{2,1,0:T(8,128)(2,1)} %copy-done.3, bf16[32,128,256]{2,1,0:T(8,128)(2,1)} %gather_fusion.1), kind=kOutput, calls=%fused_computation.43.clone.1 | convolution fusion | flops 268435456 | bytes 7340032 | tf_op jit(solution)/shard_map/while/body/eval_jaxpr/gui,gir->gur/dot_general | solution.py:30
  130.8 6.5 %scatter_fusion = f32[8,128,256]{2,1,0:T(8,128)S(1)} fusion(f32[8,128,256]{2,1,0:T(8,128)S(1)} %get-tuple-element.158, s32[32]{0:T(128)S(1)} %get-tuple-element.146, f32[32,128,256]{2,1,0:T(8,128)} %fusion.44), kind=kCustom, calls=%fused_computation.3.clone.1 | custom fusion | flops 1048576 | bytes 12583040 | tf_op jit(solution)/shard_map/while/body/eval_jaxpr/scatter-add | solution.py:36
  137.3 3.2 %gather_fusion.1 = bf16[32,128,256]{2,1,0:T(8,128)(2,1)} fusion(bf16[16,128,256]{2,1,0:T(8,128)(2,1)} %get-tuple-element.173, s32[1024]{0:T(1024)S(1)} %pad_clamp_fusion.6), kind=kCustom, calls=%fused_computation.1.clone.1 | custom fusion | bytes 4194432 | tf_op jit(solution)/shard_map/while/body/eval_jaxpr/gather | solution.py:22
  140.5 3.1 %gather_fusion = bf16[32,128,256]{2,1,0:T(8,128)(2,1)} fusion(bf16[8,128,256]{2,1,0:T(8,128)(2,1)} %get-tuple-element.171, s32[1024]{0:T(1024)S(1)} %pad_clamp_fusion.5), kind=kCustom, calls=%fused_computation.clone.1 | custom fusion | bytes 4194432 | tf_op jit(solution)/shard_map/while/body/eval_jaxpr/gather | solution.py:21
  143.6 3.4 %fusion.43 = bf16[32,128,128]{2,1,0:T(8,128)(2,1)S(1)} fusion(bf16[32,128,256]{2,1,0:T(8,128)(2,1)} %gather_fusion, bf16[32,128,256]{2,1,0:T(8,128)(2,1)} %gather_fusion.1, bf16[4,32,128,128]{3,2,1,0:T(8,128)(2,1)} %get-tuple-element.170, s32[]{:T(128)S(6)} %copy.28), kind=kOutput, calls=%fused_computation.11.clone.1 | convolution fusion | flops 273154048 | bytes 6291460 | tf_op jit(solution)/shard_map/while/body/eval_jaxpr/gur,gir->gui/dot_general | solution.py:23
  147.0 1.0 copy-done.3
  148.0 2.7 %fusion.45 = f32[32,128,256]{2,1,0:T(8,128)} fusion(bf16[32,128,128]{2,1,0:T(8,128)(2,1)S(1)} %fusion.43, bf16[32,128,256]{2,1,0:T(8,128)(2,1)S(1)} %copy-done.1), kind=kOutput, calls=%fused_computation.44.clone.1 | convolution fusion | flops 268435456 | bytes 7340032 | tf_op jit(solution)/shard_map/while/body/eval_jaxpr/gui,gur->gir/dot_general | solution.py:33
  150.7 6.5 %scatter_fusion.1 = f32[16,128,256]{2,1,0:T(8,128)S(1)} fusion(f32[16,128,256]{2,1,0:T(8,128)S(1)} %get-tuple-element.159, s32[32]{0:T(128)S(1)} %get-tuple-element.147, f32[32,128,256]{2,1,0:T(8,128)} %fusion.45), kind=kCustom, calls=%fused_computation.4.clone.1 | custom fusion | flops 1048576 | bytes 12583040 | tf_op jit(solution)/shard_map/while/body/eval_jaxpr/scatter-add | solution.py:37
  157.2 4.6 %fusion.44 = f32[32,128,256]{2,1,0:T(8,128)} fusion(bf16[32,128,128]{2,1,0:T(8,128)(2,1)} %copy-done.3, bf16[32,128,256]{2,1,0:T(8,128)(2,1)} %gather_fusion.1), kind=kOutput, calls=%fused_computation.43.clone.1 | convolution fusion | flops 268435456 | bytes 7340032 | tf_op jit(solution)/shard_map/while/body/eval_jaxpr/gui,gir->gur/dot_general | solution.py:30
  161.7 6.5 %scatter_fusion = f32[8,128,256]{2,1,0:T(8,128)S(1)} fusion(f32[8,128,256]{2,1,0:T(8,128)S(1)} %get-tuple-element.158, s32[32]{0:T(128)S(1)} %get-tuple-element.146, f32[32,128,256]{2,1,0:T(8,128)} %fusion.44), kind=kCustom, calls=%fused_computation.3.clone.1 | custom fusion | flops 1048576 | bytes 12583040 | tf_op jit(solution)/shard_map/while/body/eval_jaxpr/scatter-add | solution.py:36
  168.4 30.6 %all_to_all.10 = bf16[16,128,256]{2,1,0:T(8,128)(2,1)S(1)} all-to-all(bf16[16,128,256]{2,1,0:T(8,128)(2,1)S(1)} %convert_element_type.21), channel_id=1, replica_groups=mesh['users'=16,'rep'=2] {'users'}, dimensions={0} | all-to-all | bytes 2097152 | tf_op jit(solution)/shard_map/all_to_all | solution.py:78
  199.0 0.7 fusion.9
  199.7 0.7 copy.19
  200.4 18.4 %all-reduce.3.cloned.1.call-done = (f32[1024,256]{1,0:T(8,128)}, f32[256,256]{1,0:T(8,128)}) async-done(((f32[1024,256]{1,0:T(8,128)}, f32[256,256]{1,0:T(8,128)}), (f32[1024,256]{1,0:T(8,128)}, f32[256,256]{1,0:T(8,128)})) %all-reduce.3.cloned.1.call-update) | async-done | bytes 1310736 | tf_op jit(solution)/shard_map/psum | solution.py:86
  218.8 1.8 multiply_subtract_fusion.1
  220.6 2.7 %multiply_subtract_fusion = (f32[1024,256]{1,0:T(8,128)}, f32[1024,256]{1,0:T(8,128)}) fusion(f32[1024,256]{1,0:T(8,128)S(1)} %copy-done.5, f32[1024,256]{1,0:T(8,128)} %get-tuple-element.87, f32[1024,256]{1,0:T(8,128)S(1)} %copy-done.6), kind=kLoop, calls=%fused_computation.25 | loop fusion | flops 1048576 | bytes 5242880 | tf_op jit(solution)/shard_map/sub | solution.py:56
  (53 shorter events, 1.3 us)
Async XLA Ops:
  8.8 10.5 %copy-start.10 = (s32[1,1,128]{2,1,0:T(1,128)S(1)}, s32[1,1,128]{2,1,0:T(1,128)}, u32[]{:S(2)}) copy-start(s32[1,1,128]{2,1,0:T(1,128)} %param.15) | copy-start | bytes 1540
  8.8 11.2 %copy-start.11 = (s32[1,1,128]{2,1,0:T(1,128)S(1)}, s32[1,1,128]{2,1,0:T(1,128)}, u32[]{:S(2)}) copy-start(s32[1,1,128]{2,1,0:T(1,128)} %param.16) | copy-start | bytes 1540
  8.8 12.0 %copy-start.4 = (f32[1024,256]{1,0:T(8,128)S(1)}, f32[1024,256]{1,0:T(8,128)}, u32[]{:S(2)}) copy-start(f32[1024,256]{1,0:T(8,128)} %param.10) | copy-start | bytes 3145732
  10.4 32.7 %all-to-all-start = ((bf16[16,128,256]{2,1,0:T(8,128)(2,1)}), bf16[16,128,256]{2,1,0:T(8,128)(2,1)S(1)}, u32[]{:S(2)}, u32[]{:S(2)}) async-start(bf16[16,128,256]{2,1,0:T(8,128)(2,1)} %gather_fusion.2), calls=%async_computation | async-start | bytes 2097152 | tf_op jit(solution)/shard_map/all_to_all | solution.py:74
  18.8 200.0 %all-reduce.3.cloned.1.call-start = ((), (), s32[]{:S(2)}) async-start(), calls=%async_computation.2 | async-start | bytes 2621440 | tf_op jit(solution)/shard_map/psum | solution.py:86
  43.2 1.0 copy-start.2
  50.8 4.4 %copy-start.1 = (bf16[32,128,256]{2,1,0:T(8,128)(2,1)S(1)}, bf16[32,128,256]{2,1,0:T(8,128)(2,1)}, u32[]{:S(2)}) copy-start(bf16[32,128,256]{2,1,0:T(8,128)(2,1)} %gather_fusion) | copy-start | bytes 6291460 | tf_op jit(solution)/shard_map/while
  54.2 1.0 copy-start.3
  81.7 4.4 %copy-start.1 = (bf16[32,128,256]{2,1,0:T(8,128)(2,1)S(1)}, bf16[32,128,256]{2,1,0:T(8,128)(2,1)}, u32[]{:S(2)}) copy-start(bf16[32,128,256]{2,1,0:T(8,128)(2,1)} %gather_fusion) | copy-start | bytes 6291460 | tf_op jit(solution)/shard_map/while
  85.1 1.0 copy-start.3
  112.7 4.4 %copy-start.1 = (bf16[32,128,256]{2,1,0:T(8,128)(2,1)S(1)}, bf16[32,128,256]{2,1,0:T(8,128)(2,1)}, u32[]{:S(2)}) copy-start(bf16[32,128,256]{2,1,0:T(8,128)(2,1)} %gather_fusion) | copy-start | bytes 6291460 | tf_op jit(solution)/shard_map/while
  116.1 1.0 copy-start.3
  143.6 4.4 %copy-start.1 = (bf16[32,128,256]{2,1,0:T(8,128)(2,1)S(1)}, bf16[32,128,256]{2,1,0:T(8,128)(2,1)}, u32[]{:S(2)}) copy-start(bf16[32,128,256]{2,1,0:T(8,128)(2,1)} %gather_fusion) | copy-start | bytes 6291460 | tf_op jit(solution)/shard_map/while
  147.0 1.0 copy-start.3
  168.2 30.8 %copy-start = (f32[8,128,256]{2,1,0:T(8,128)}, f32[8,128,256]{2,1,0:T(8,128)S(1)}, u32[]{:S(2)}) copy-start(f32[8,128,256]{2,1,0:T(8,128)S(1)} %get-tuple-element.69) | copy-start | bytes 3145732
  168.2 30.8 %copy-start.9 = (s32[1,1,16]{2,1,0:T(1,128)S(1)}, s32[1,1,16]{2,1,0:T(1,128)}, u32[]{:S(2)}) copy-start(s32[1,1,16]{2,1,0:T(1,128)} %param.17) | copy-start | bytes 196
  199.0 19.9 %copy-start.7 = (f32[256,256]{1,0:T(8,128)S(1)}, f32[256,256]{1,0:T(8,128)}, u32[]{:S(2)}) copy-start(f32[256,256]{1,0:T(8,128)} %param.12) | copy-start | bytes 786436
  199.0 19.9 %copy-start.8 = (f32[256,256]{1,0:T(8,128)S(1)}, f32[256,256]{1,0:T(8,128)}, u32[]{:S(2)}) copy-start(f32[256,256]{1,0:T(8,128)} %param.13) | copy-start | bytes 786436
  199.0 21.6 %copy-start.5 = (f32[1024,256]{1,0:T(8,128)S(1)}, f32[1024,256]{1,0:T(8,128)}, u32[]{:S(2)}) copy-start(f32[1024,256]{1,0:T(8,128)} %param.10) | copy-start | bytes 3145732
  199.0 21.6 %copy-start.6 = (f32[1024,256]{1,0:T(8,128)S(1)}, f32[1024,256]{1,0:T(8,128)}, u32[]{:S(2)}) copy-start(f32[1024,256]{1,0:T(8,128)} %param.11) | copy-start | bytes 3145732
Sparse Core Ops, SparseCore 0:
  200.5 18.2 all-reduce.2
where the time goes:
time: 231 us; the launch traced here: 230 us
  other arithmetic  60.3 us (26%)
  matrix products  43.3 us (19%)
  waiting for transfers between devices  39.9 us (17%)
  local copies, waits for them, and re-layouts  33.3 us (14%)
  blocking collectives  30.6 us (13%)
  between operations  14.1 us (6%)
  starting transfers between devices  8.38 us (4%)
    all_to_all x1, blocking collectives, local(): lax.all_to_all(slot_part.astype(jnp.bfloat16), 'users', split_axis=0, con...  30.6 us
    scatter-add x4, other arithmetic, tile_step(): slot_total = slot_total.at[block_slot].add(item_part)  25.9 us
    scatter-add x4, other arithmetic, tile_step(): user_total = user_total.at[block_user].add(user_part)  25.8 us
    all_to_all x1, waiting for transfers between devices, local(): lax.all_to_all(outgoing, 'users', split_axis=0, concat_axis=0, tiled=True)  21.4 us
    psum x1, waiting for transfers between devices, local(): user_grad = lax.psum(user_part.reshape(-1, feat_width), 'rep')  18.4 us
    dot_general x4, matrix products, tile_step(): jnp.einsum('gui,gir->gur', weighted_err, item_rows, preferred_element_typ...  18.2 us
    dot_general x4, matrix products, tile_step(): jnp.einsum('gur,gir->gui', user_rows, item_rows, preferred_element_type=j...  13.6 us
    gather x4, local copies, waits for them, and re-layouts, tile_step(): item_rows = panels[block_fetch]  12.9 us
  transfers between devices with their start and end apart: 2, of which 2 were waited for; matrix products, arithmetic and copies ran while one was open for 1% of the time, Pallas kernels for 0%

commit v1 on v0

--- a/solution.py
+++ b/solution.py
@@ -71,7 +71,19 @@
     send_row = send_list[0, 0]
     slot_index = items_idx // panels_own
     outgoing = owned_panels[jnp.minimum(send_row, panels_own - 1)]
-    panels = lax.all_to_all(outgoing, "users", split_axis=0, concat_axis=0, tiled=True)
+    ways, here = (lax.axis_size("users"), lax.axis_index("users"))
+    width_2 = outgoing.shape[0] // ways
+    lengths = list(outgoing.shape)
+    lengths[0] = width_2
+    height = lengths[0]
+    lengths[0] = height * ways
+    full = jnp.zeros(lengths, outgoing.dtype)
+    for mask in range(ways):
+        part = lax.dynamic_slice_in_dim(outgoing, (here ^ mask) * width_2, width_2, axis=0)
+        if mask:
+            part = lax.ppermute(part, "users", [(d, d ^ mask) for d in range(ways)])
+        full = lax.dynamic_update_slice_in_dim(full, part, (here ^ mask) * height, axis=0)
+    panels = full
     user_part, slot_part = tile_terms(
         user_strip, panels, counts, users_idx, slot_index, slot_index, peer_count
     )

time: 231 us -> 264 us (1.14)
  starting transfers between devices: 8.38 us -> 32.3 us
  waiting for transfers between devices: 39.9 us -> 54.8 us
  blocking collectives: 30.6 us -> 24.1 us
    ppermute x0 -> x15, waiting for transfers between devices: none -> 36.4 us  [local(): part = lax.ppermute(part, 'users', [(d, d ^ mask) for d in range(ways)])]
    ppermute x0 -> x15, starting transfers between devices: none -> 32.2 us  [local(): part = lax.ppermute(part, 'users', [(d, d ^ mask) for d in range(ways)])]
    all_to_all x1 -> x0, waiting for transfers between devices: 21.4 us -> none  [local(): lax.all_to_all(outgoing, 'users', split_axis=0, concat_axis=0, tiled=True)]
    all_to_all x1 -> x0, starting transfers between devices: 8.34 us -> none  [local(): lax.all_to_all(outgoing, 'users', split_axis=0, concat_axis=0, tiled=True)]
    all_to_all x1, blocking collectives: 30.6 us -> 24.1 us  [local(): lax.all_to_all(slot_part.astype(jnp.bfloat16), 'users', split_axis=0, con...]
  transfers between devices with their start and end apart: 2 -> 16, of which waited for: 2 -> 12; matrix products, arithmetic and copies ran while one was open for 1% -> 1% of each run, Pallas kernels for 0% -> 0%
where the time goes in v1:
time: 264 us; the launch traced here: 263 us
  other arithmetic  60.1 us (23%)
  waiting for transfers between devices  54.8 us (21%)
  matrix products  43.3 us (16%)
  local copies, waits for them, and re-layouts  33.5 us (13%)
  starting transfers between devices  32.3 us (12%)
  blocking collectives  24.1 us (9%)
  between operations  14.4 us (5%)
    ppermute x15, waiting for transfers between devices, local(): part = lax.ppermute(part, 'users', [(d, d ^ mask) for d in range(ways)])  36.4 us
    ppermute x15, starting transfers between devices, local(): part = lax.ppermute(part, 'users', [(d, d ^ mask) for d in range(ways)])  32.2 us
    scatter-add x4, other arithmetic, tile_step(): slot_total = slot_total.at[block_slot].add(item_part)  25.9 us
    scatter-add x4, other arithmetic, tile_step(): user_total = user_total.at[block_user].add(user_part)  25.8 us
    all_to_all x1, blocking collectives, local(): lax.all_to_all(slot_part.astype(jnp.bfloat16), 'users', split_axis=0, con...  24.1 us
    psum x1, waiting for transfers between devices, local(): user_grad = lax.psum(user_part.reshape(-1, feat_width), 'rep')  18.4 us
    dot_general x4, matrix products, tile_step(): jnp.einsum('gui,gir->gur', weighted_err, item_rows, preferred_element_typ...  18.2 us
    dot_general x4, matrix products, tile_step(): jnp.einsum('gur,gir->gui', user_rows, item_rows, preferred_element_type=j...  13.6 us
  transfers between devices with their start and end apart: 16, of which 12 were waited for; matrix products, arithmetic and copies ran while one was open for 1% of the time, Pallas kernels for 0%

profile of v1, /device:TPU:0, one launch (start us, length us, event | category | flops | bytes accessed | tf_op | source)
XLA Modules:
  0.0 262.9 jit_solution(4171380172794351859)
XLA Ops:
  10.7 7.0 %collective-permute-start.14 = (bf16[1,128,256]{2,1,0:T(8,128)(2,1)S(1)}, bf16[1,128,256]{2,1,0:T(8,128)(2,1)S(1)}, u32[]{:S(2)}, u32[]{:S(2)}) collective-permute-start(bf16[1,128,256]{2,1,0:T(8,128)(2,1)S(1)} %get-tuple-element.95), channel_id=1, source_target_pairs={{0,30},{2,28},{4,26},{6,24},{8,22},{10,20},{12,18},{14,16},{16,14}... | collective-permute-start | bytes 196616 | tf_op jit(solution)/shard_map/ppermute | solution.py:84
  17.8 3.6 %collective-permute-start.12 = (bf16[1,128,256]{2,1,0:T(8,128)(2,1)S(1)}, bf16[1,128,256]{2,1,0:T(8,128)(2,1)S(1)}, u32[]{:S(2)}, u32[]{:S(2)}) collective-permute-start(bf16[1,128,256]{2,1,0:T(8,128)(2,1)S(1)} %get-tuple-element.97), channel_id=1, source_target_pairs={{0,26},{2,24},{4,30},{6,28},{8,18},{10,16},{12,22},{14,20},{16,10}... | collective-permute-start | bytes 196616 | tf_op jit(solution)/shard_map/ppermute | solution.py:84
  27.6 2.9 %collective-permute-done.1 = bf16[1,128,256]{2,1,0:T(8,128)(2,1)S(1)} collective-permute-done((bf16[1,128,256]{2,1,0:T(8,128)(2,1)}, bf16[1,128,256]{2,1,0:T(8,128)(2,1)S(1)}, u32[]{:S(2)}, u32[]{:S(2)}) %collective-permute-start.1) | collective-permute-done | bytes 65568 | tf_op jit(solution)/shard_map/ppermute | solution.py:84
  30.5 2.5 collective-permute-start.2
  33.1 2.9 %collective-permute-done.2 = bf16[1,128,256]{2,1,0:T(8,128)(2,1)S(1)} collective-permute-done((bf16[1,128,256]{2,1,0:T(8,128)(2,1)}, bf16[1,128,256]{2,1,0:T(8,128)(2,1)S(1)}, u32[]{:S(2)}, u32[]{:S(2)}) %collective-permute-start.2) | collective-permute-done | bytes 65568 | tf_op jit(solution)/shard_map/ppermute | solution.py:84
  35.9 4.9 %collective-permute-done.3 = bf16[1,128,256]{2,1,0:T(8,128)(2,1)S(1)} collective-permute-done((bf16[1,128,256]{2,1,0:T(8,128)(2,1)}, bf16[1,128,256]{2,1,0:T(8,128)(2,1)S(1)}, u32[]{:S(2)}, u32[]{:S(2)}) %collective-permute-start.3) | collective-permute-done | bytes 65568 | tf_op jit(solution)/shard_map/ppermute | solution.py:84
  41.4 4.8 %collective-permute-done.4 = bf16[1,128,256]{2,1,0:T(8,128)(2,1)S(1)} collective-permute-done((bf16[1,128,256]{2,1,0:T(8,128)(2,1)}, bf16[1,128,256]{2,1,0:T(8,128)(2,1)S(1)}, u32[]{:S(2)}, u32[]{:S(2)}) %collective-permute-start.4) | collective-permute-done | bytes 65568 | tf_op jit(solution)/shard_map/ppermute | solution.py:84
  47.2 4.2 %collective-permute-done.5 = bf16[1,128,256]{2,1,0:T(8,128)(2,1)S(1)} collective-permute-done((bf16[1,128,256]{2,1,0:T(8,128)(2,1)S(1)}, bf16[1,128,256]{2,1,0:T(8,128)(2,1)S(1)}, u32[]{:S(2)}, u32[]{:S(2)}) %collective-permute-start.5) | collective-permute-done | bytes 65568 | tf_op jit(solution)/shard_map/ppermute | solution.py:84
  52.9 4.5 %collective-permute-done.6 = bf16[1,128,256]{2,1,0:T(8,128)(2,1)S(1)} collective-permute-done((bf16[1,128,256]{2,1,0:T(8,128)(2,1)S(1)}, bf16[1,128,256]{2,1,0:T(8,128)(2,1)S(1)}, u32[]{:S(2)}, u32[]{:S(2)}) %collective-permute-start.6) | collective-permute-done | bytes 65568 | tf_op jit(solution)/shard_map/ppermute | solution.py:84
  57.4 2.4 collective-permute-start.7
  59.9 2.7 %collective-permute-done.7 = bf16[1,128,256]{2,1,0:T(8,128)(2,1)S(1)} collective-permute-done((bf16[1,128,256]{2,1,0:T(8,128)(2,1)S(1)}, bf16[1,128,256]{2,1,0:T(8,128)(2,1)S(1)}, u32[]{:S(2)}, u32[]{:S(2)}) %collective-permute-start.7) | collective-permute-done | bytes 65568 | tf_op jit(solution)/shard_map/ppermute | solution.py:84
  62.6 2.8 %collective-permute-start.8 = (bf16[1,128,256]{2,1,0:T(8,128)(2,1)S(1)}, bf16[1,128,256]{2,1,0:T(8,128)(2,1)S(1)}, u32[]{:S(2)}, u32[]{:S(2)}) collective-permute-start(bf16[1,128,256]{2,1,0:T(8,128)(2,1)S(1)} %copy-done.9), channel_id=1, source_target_pairs={{0,18},{2,16},{4,22},{6,20},{8,26},{10,24},{12,30},{14,28},{16,2},... | collective-permute-start | bytes 196616 | tf_op jit(solution)/shard_map/ppermute | solution.py:84
  65.4 3.3 %collective-permute-done.8 = bf16[1,128,256]{2,1,0:T(8,128)(2,1)S(1)} collective-permute-done((bf16[1,128,256]{2,1,0:T(8,128)(2,1)S(1)}, bf16[1,128,256]{2,1,0:T(8,128)(2,1)S(1)}, u32[]{:S(2)}, u32[]{:S(2)}) %collective-permute-start.8) | collective-permute-done | bytes 65568 | tf_op jit(solution)/shard_map/ppermute | solution.py:84
  68.7 4.2 %collective-permute-start.9 = (bf16[1,128,256]{2,1,0:T(8,128)(2,1)S(1)}, bf16[1,128,256]{2,1,0:T(8,128)(2,1)S(1)}, u32[]{:S(2)}, u32[]{:S(2)}) collective-permute-start(bf16[1,128,256]{2,1,0:T(8,128)(2,1)S(1)} %get-tuple-element.100), channel_id=1, source_target_pairs={{0,20},{2,22},{4,16},{6,18},{8,28},{10,30},{12,24},{14,26},{16,4},... | collective-permute-start | bytes 196616 | tf_op jit(solution)/shard_map/ppermute | solution.py:84
  75.1 3.3 %collective-permute-start.10 = (bf16[1,128,256]{2,1,0:T(8,128)(2,1)S(1)}, bf16[1,128,256]{2,1,0:T(8,128)(2,1)S(1)}, u32[]{:S(2)}, u32[]{:S(2)}) collective-permute-start(bf16[1,128,256]{2,1,0:T(8,128)(2,1)S(1)} %get-tuple-element.99), channel_id=1, source_target_pairs={{0,22},{2,20},{4,18},{6,16},{8,30},{10,28},{12,26},{14,24},{16,6},... | collective-permute-start | bytes 196616 | tf_op jit(solution)/shard_map/ppermute | solution.py:84
  78.4 3.7 %collective-permute-done.10 = bf16[1,128,256]{2,1,0:T(8,128)(2,1)S(1)} collective-permute-done((bf16[1,128,256]{2,1,0:T(8,128)(2,1)S(1)}, bf16[1,128,256]{2,1,0:T(8,128)(2,1)S(1)}, u32[]{:S(2)}, u32[]{:S(2)}) %collective-permute-start.10) | collective-permute-done | bytes 65568 | tf_op jit(solution)/shard_map/ppermute | solution.py:84
  83.5 123.9 %while.13 = (s32[]{:T(128)}, f32[8,128,256]{2,1,0:T(8,128)S(1)}, f32[16,128,256]{2,1,0:T(8,128)S(1)}, s32[4,32]{1,0:T(4,128)S(1)}, bf16[4,32,128,128]{3,2,1,0:T(...) while((s32[]{:T(128)}, f32[8,128,256]{2,1,0:T(8,128)S(1)}, ...), condition=%wide.region_3.4_spmd, body=%wide.region_0.3_spmd.sunk | while | flops 812124352 | bytes 67118496 | solution.py:50
  83.5 3.3 %gather_fusion.1 = bf16[32,128,256]{2,1,0:T(8,128)(2,1)} fusion(bf16[16,128,256]{2,1,0:T(8,128)(2,1)} %get-tuple-element.189, s32[1024]{0:T(1024)S(1)} %pad_clamp_fusion.6), kind=kCustom, calls=%fused_computation.1.clone.1 | custom fusion | bytes 4194432 | tf_op jit(solution)/shard_map/while/body/eval_jaxpr/gather | solution.py:22
  86.8 3.0 %gather_fusion = bf16[32,128,256]{2,1,0:T(8,128)(2,1)} fusion(bf16[8,128,256]{2,1,0:T(8,128)(2,1)} %get-tuple-element.187, s32[1024]{0:T(1024)S(1)} %pad_clamp_fusion.5), kind=kCustom, calls=%fused_computation.clone.1 | custom fusion | bytes 4194432 | tf_op jit(solution)/shard_map/while/body/eval_jaxpr/gather | solution.py:21
  89.8 3.4 %fusion.43 = bf16[32,128,128]{2,1,0:T(8,128)(2,1)S(1)} fusion(bf16[32,128,256]{2,1,0:T(8,128)(2,1)} %gather_fusion, bf16[32,128,256]{2,1,0:T(8,128)(2,1)} %gather_fusion.1, bf16[4,32,128,128]{3,2,1,0:T(8,128)(2,1)} %get-tuple-element.186, s32[]{:T(128)S(6)} %copy.44), kind=kOutput, calls=%fused_computation.11.clone.1 | convolution fusion | flops 273154048 | bytes 6291460 | tf_op jit(solution)/shard_map/while/body/eval_jaxpr/gur,gir->gui/dot_general | solution.py:23
  94.2 2.7 %fusion.45 = f32[32,128,256]{2,1,0:T(8,128)} fusion(bf16[32,128,128]{2,1,0:T(8,128)(2,1)S(1)} %fusion.43, bf16[32,128,256]{2,1,0:T(8,128)(2,1)S(1)} %copy-done.1), kind=kOutput, calls=%fused_computation.75.clone.1 | convolution fusion | flops 268435456 | bytes 7340032 | tf_op jit(solution)/shard_map/while/body/eval_jaxpr/gui,gur->gir/dot_general | solution.py:33
  96.9 6.5 %scatter_fusion.1 = f32[16,128,256]{2,1,0:T(8,128)S(1)} fusion(f32[16,128,256]{2,1,0:T(8,128)S(1)} %get-tuple-element.175, s32[32]{0:T(128)S(1)} %get-tuple-element.163, f32[32,128,256]{2,1,0:T(8,128)} %fusion.45), kind=kCustom, calls=%fused_computation.4.clone.1 | custom fusion | flops 1048576 | bytes 12583040 | tf_op jit(solution)/shard_map/while/body/eval_jaxpr/scatter-add | solution.py:37
  103.4 4.6 %fusion.44 = f32[32,128,256]{2,1,0:T(8,128)} fusion(bf16[32,128,128]{2,1,0:T(8,128)(2,1)} %copy-done.3, bf16[32,128,256]{2,1,0:T(8,128)(2,1)} %gather_fusion.1), kind=kOutput, calls=%fused_computation.74.clone.1 | convolution fusion | flops 268435456 | bytes 7340032 | tf_op jit(solution)/shard_map/while/body/eval_jaxpr/gui,gir->gur/dot_general | solution.py:30
  108.0 6.5 %scatter_fusion = f32[8,128,256]{2,1,0:T(8,128)S(1)} fusion(f32[8,128,256]{2,1,0:T(8,128)S(1)} %get-tuple-element.174, s32[32]{0:T(128)S(1)} %get-tuple-element.162, f32[32,128,256]{2,1,0:T(8,128)} %fusion.44), kind=kCustom, calls=%fused_computation.3.clone.1 | custom fusion | flops 1048576 | bytes 12583040 | tf_op jit(solution)/shard_map/while/body/eval_jaxpr/scatter-add | solution.py:36
  114.5 3.3 %gather_fusion.1 = bf16[32,128,256]{2,1,0:T(8,128)(2,1)} fusion(bf16[16,128,256]{2,1,0:T(8,128)(2,1)} %get-tuple-element.189, s32[1024]{0:T(1024)S(1)} %pad_clamp_fusion.6), kind=kCustom, calls=%fused_computation.1.clone.1 | custom fusion | bytes 4194432 | tf_op jit(solution)/shard_map/while/body/eval_jaxpr/gather | solution.py:22
  117.8 3.0 %gather_fusion = bf16[32,128,256]{2,1,0:T(8,128)(2,1)} fusion(bf16[8,128,256]{2,1,0:T(8,128)(2,1)} %get-tuple-element.187, s32[1024]{0:T(1024)S(1)} %pad_clamp_fusion.5), kind=kCustom, calls=%fused_computation.clone.1 | custom fusion | bytes 4194432 | tf_op jit(solution)/shard_map/while/body/eval_jaxpr/gather | solution.py:21
  120.8 3.4 %fusion.43 = bf16[32,128,128]{2,1,0:T(8,128)(2,1)S(1)} fusion(bf16[32,128,256]{2,1,0:T(8,128)(2,1)} %gather_fusion, bf16[32,128,256]{2,1,0:T(8,128)(2,1)} %gather_fusion.1, bf16[4,32,128,128]{3,2,1,0:T(8,128)(2,1)} %get-tuple-element.186, s32[]{:T(128)S(6)} %copy.44), kind=kOutput, calls=%fused_computation.11.clone.1 | convolution fusion | flops 273154048 | bytes 6291460 | tf_op jit(solution)/shard_map/while/body/eval_jaxpr/gur,gir->gui/dot_general | solution.py:23
  125.2 2.7 %fusion.45 = f32[32,128,256]{2,1,0:T(8,128)} fusion(bf16[32,128,128]{2,1,0:T(8,128)(2,1)S(1)} %fusion.43, bf16[32,128,256]{2,1,0:T(8,128)(2,1)S(1)} %copy-done.1), kind=kOutput, calls=%fused_computation.75.clone.1 | convolution fusion | flops 268435456 | bytes 7340032 | tf_op jit(solution)/shard_map/while/body/eval_jaxpr/gui,gur->gir/dot_general | solution.py:33
  127.9 6.5 %scatter_fusion.1 = f32[16,128,256]{2,1,0:T(8,128)S(1)} fusion(f32[16,128,256]{2,1,0:T(8,128)S(1)} %get-tuple-element.175, s32[32]{0:T(128)S(1)} %get-tuple-element.163, f32[32,128,256]{2,1,0:T(8,128)} %fusion.45), kind=kCustom, calls=%fused_computation.4.clone.1 | custom fusion | flops 1048576 | bytes 12583040 | tf_op jit(solution)/shard_map/while/body/eval_jaxpr/scatter-add | solution.py:37
  134.4 4.6 %fusion.44 = f32[32,128,256]{2,1,0:T(8,128)} fusion(bf16[32,128,128]{2,1,0:T(8,128)(2,1)} %copy-done.3, bf16[32,128,256]{2,1,0:T(8,128)(2,1)} %gather_fusion.1), kind=kOutput, calls=%fused_computation.74.clone.1 | convolution fusion | flops 268435456 | bytes 7340032 | tf_op jit(solution)/shard_map/while/body/eval_jaxpr/gui,gir->gur/dot_general | solution.py:30
  138.9 6.5 %scatter_fusion = f32[8,128,256]{2,1,0:T(8,128)S(1)} fusion(f32[8,128,256]{2,1,0:T(8,128)S(1)} %get-tuple-element.174, s32[32]{0:T(128)S(1)} %get-tuple-element.162, f32[32,128,256]{2,1,0:T(8,128)} %fusion.44), kind=kCustom, calls=%fused_computation.3.clone.1 | custom fusion | flops 1048576 | bytes 12583040 | tf_op jit(solution)/shard_map/while/body/eval_jaxpr/scatter-add | solution.py:36
  145.5 3.3 %gather_fusion.1 = bf16[32,128,256]{2,1,0:T(8,128)(2,1)} fusion(bf16[16,128,256]{2,1,0:T(8,128)(2,1)} %get-tuple-element.189, s32[1024]{0:T(1024)S(1)} %pad_clamp_fusion.6), kind=kCustom, calls=%fused_computation.1.clone.1 | custom fusion | bytes 4194432 | tf_op jit(solution)/shard_map/while/body/eval_jaxpr/gather | solution.py:22
  148.7 3.0 %gather_fusion = bf16[32,128,256]{2,1,0:T(8,128)(2,1)} fusion(bf16[8,128,256]{2,1,0:T(8,128)(2,1)} %get-tuple-element.187, s32[1024]{0:T(1024)S(1)} %pad_clamp_fusion.5), kind=kCustom, calls=%fused_computation.clone.1 | custom fusion | bytes 4194432 | tf_op jit(solution)/shard_map/while/body/eval_jaxpr/gather | solution.py:21
  151.8 3.4 %fusion.43 = bf16[32,128,128]{2,1,0:T(8,128)(2,1)S(1)} fusion(bf16[32,128,256]{2,1,0:T(8,128)(2,1)} %gather_fusion, bf16[32,128,256]{2,1,0:T(8,128)(2,1)} %gather_fusion.1, bf16[4,32,128,128]{3,2,1,0:T(8,128)(2,1)} %get-tuple-element.186, s32[]{:T(128)S(6)} %copy.44), kind=kOutput, calls=%fused_computation.11.clone.1 | convolution fusion | flops 273154048 | bytes 6291460 | tf_op jit(solution)/shard_map/while/body/eval_jaxpr/gur,gir->gui/dot_general | solution.py:23
  156.2 2.7 %fusion.45 = f32[32,128,256]{2,1,0:T(8,128)} fusion(bf16[32,128,128]{2,1,0:T(8,128)(2,1)S(1)} %fusion.43, bf16[32,128,256]{2,1,0:T(8,128)(2,1)S(1)} %copy-done.1), kind=kOutput, calls=%fused_computation.75.clone.1 | convolution fusion | flops 268435456 | bytes 7340032 | tf_op jit(solution)/shard_map/while/body/eval_jaxpr/gui,gur->gir/dot_general | solution.py:33
  158.9 6.5 %scatter_fusion.1 = f32[16,128,256]{2,1,0:T(8,128)S(1)} fusion(f32[16,128,256]{2,1,0:T(8,128)S(1)} %get-tuple-element.175, s32[32]{0:T(128)S(1)} %get-tuple-element.163, f32[32,128,256]{2,1,0:T(8,128)} %fusion.45), kind=kCustom, calls=%fused_computation.4.clone.1 | custom fusion | flops 1048576 | bytes 12583040 | tf_op jit(solution)/shard_map/while/body/eval_jaxpr/scatter-add | solution.py:37
  165.4 4.6 %fusion.44 = f32[32,128,256]{2,1,0:T(8,128)} fusion(bf16[32,128,128]{2,1,0:T(8,128)(2,1)} %copy-done.3, bf16[32,128,256]{2,1,0:T(8,128)(2,1)} %gather_fusion.1), kind=kOutput, calls=%fused_computation.74.clone.1 | convolution fusion | flops 268435456 | bytes 7340032 | tf_op jit(solution)/shard_map/while/body/eval_jaxpr/gui,gir->gur/dot_general | solution.py:30
  169.9 6.5 %scatter_fusion = f32[8,128,256]{2,1,0:T(8,128)S(1)} fusion(f32[8,128,256]{2,1,0:T(8,128)S(1)} %get-tuple-element.174, s32[32]{0:T(128)S(1)} %get-tuple-element.162, f32[32,128,256]{2,1,0:T(8,128)} %fusion.44), kind=kCustom, calls=%fused_computation.3.clone.1 | custom fusion | flops 1048576 | bytes 12583040 | tf_op jit(solution)/shard_map/while/body/eval_jaxpr/scatter-add | solution.py:36
  176.4 3.3 %gather_fusion.1 = bf16[32,128,256]{2,1,0:T(8,128)(2,1)} fusion(bf16[16,128,256]{2,1,0:T(8,128)(2,1)} %get-tuple-element.189, s32[1024]{0:T(1024)S(1)} %pad_clamp_fusion.6), kind=kCustom, calls=%fused_computation.1.clone.1 | custom fusion | bytes 4194432 | tf_op jit(solution)/shard_map/while/body/eval_jaxpr/gather | solution.py:22
  179.7 3.0 %gather_fusion = bf16[32,128,256]{2,1,0:T(8,128)(2,1)} fusion(bf16[8,128,256]{2,1,0:T(8,128)(2,1)} %get-tuple-element.187, s32[1024]{0:T(1024)S(1)} %pad_clamp_fusion.5), kind=kCustom, calls=%fused_computation.clone.1 | custom fusion | bytes 4194432 | tf_op jit(solution)/shard_map/while/body/eval_jaxpr/gather | solution.py:21
  182.8 3.4 %fusion.43 = bf16[32,128,128]{2,1,0:T(8,128)(2,1)S(1)} fusion(bf16[32,128,256]{2,1,0:T(8,128)(2,1)} %gather_fusion, bf16[32,128,256]{2,1,0:T(8,128)(2,1)} %gather_fusion.1, bf16[4,32,128,128]{3,2,1,0:T(8,128)(2,1)} %get-tuple-element.186, s32[]{:T(128)S(6)} %copy.44), kind=kOutput, calls=%fused_computation.11.clone.1 | convolution fusion | flops 273154048 | bytes 6291460 | tf_op jit(solution)/shard_map/while/body/eval_jaxpr/gur,gir->gui/dot_general | solution.py:23
  187.2 2.7 %fusion.45 = f32[32,128,256]{2,1,0:T(8,128)} fusion(bf16[32,128,128]{2,1,0:T(8,128)(2,1)S(1)} %fusion.43, bf16[32,128,256]{2,1,0:T(8,128)(2,1)S(1)} %copy-done.1), kind=kOutput, calls=%fused_computation.75.clone.1 | convolution fusion | flops 268435456 | bytes 7340032 | tf_op jit(solution)/shard_map/while/body/eval_jaxpr/gui,gur->gir/dot_general | solution.py:33
  189.9 6.5 %scatter_fusion.1 = f32[16,128,256]{2,1,0:T(8,128)S(1)} fusion(f32[16,128,256]{2,1,0:T(8,128)S(1)} %get-tuple-element.175, s32[32]{0:T(128)S(1)} %get-tuple-element.163, f32[32,128,256]{2,1,0:T(8,128)} %fusion.45), kind=kCustom, calls=%fused_computation.4.clone.1 | custom fusion | flops 1048576 | bytes 12583040 | tf_op jit(solution)/shard_map/while/body/eval_jaxpr/scatter-add | solution.py:37
  196.3 4.6 %fusion.44 = f32[32,128,256]{2,1,0:T(8,128)} fusion(bf16[32,128,128]{2,1,0:T(8,128)(2,1)} %copy-done.3, bf16[32,128,256]{2,1,0:T(8,128)(2,1)} %gather_fusion.1), kind=kOutput, calls=%fused_computation.74.clone.1 | convolution fusion | flops 268435456 | bytes 7340032 | tf_op jit(solution)/shard_map/while/body/eval_jaxpr/gui,gir->gur/dot_general | solution.py:30
  200.9 6.5 %scatter_fusion = f32[8,128,256]{2,1,0:T(8,128)S(1)} fusion(f32[8,128,256]{2,1,0:T(8,128)S(1)} %get-tuple-element.174, s32[32]{0:T(128)S(1)} %get-tuple-element.162, f32[32,128,256]{2,1,0:T(8,128)} %fusion.44), kind=kCustom, calls=%fused_computation.3.clone.1 | custom fusion | flops 1048576 | bytes 12583040 | tf_op jit(solution)/shard_map/while/body/eval_jaxpr/scatter-add | solution.py:36
  207.5 24.1 %all_to_all.5 = bf16[16,128,256]{2,1,0:T(8,128)(2,1)S(1)} all-to-all(bf16[16,128,256]{2,1,0:T(8,128)(2,1)S(1)} %convert_element_type.21), channel_id=1, replica_groups=mesh['users'=16,'rep'=2] {'users'}, dimensions={0} | all-to-all | bytes 2097152 | tf_op jit(solution)/shard_map/all_to_all | solution.py:90
  233.1 18.4 %all-reduce.3.cloned.1.call-done = (f32[1024,256]{1,0:T(8,128)}, f32[256,256]{1,0:T(8,128)}) async-done(((f32[1024,256]{1,0:T(8,128)}, f32[256,256]{1,0:T(8,128)}), (f32[1024,256]{1,0:T(8,128)}, f32[256,256]{1,0:T(8,128)})) %all-reduce.3.cloned.1.call-update) | async-done | bytes 1310736 | tf_op jit(solution)/shard_map/psum | solution.py:98
  253.3 2.7 %multiply_subtract_fusion = (f32[1024,256]{1,0:T(8,128)}, f32[1024,256]{1,0:T(8,128)}) fusion(f32[1024,256]{1,0:T(8,128)S(1)} %copy-done.5, f32[1024,256]{1,0:T(8,128)} %get-tuple-element.87, f32[1024,256]{1,0:T(8,128)S(1)} %copy-done.6), kind=kLoop, calls=%fused_computation.25 | loop fusion | flops 1048576 | bytes 5242880 | tf_op jit(solution)/shard_map/sub | solution.py:56
  (106 shorter events, 23.6 us)
Async XLA Ops:
  7.2 244.3 %all-reduce.3.cloned.1.call-start = ((), (), s32[]{:S(2)}) async-start(), calls=%async_computation.1 | async-start | bytes 2621440 | tf_op jit(solution)/shard_map/psum | solution.py:98
  9.6 14.0 %copy-start.14 = (s32[1,1,128]{2,1,0:T(1,128)S(1)}, s32[1,1,128]{2,1,0:T(1,128)}, u32[]{:S(2)}) copy-start(s32[1,1,128]{2,1,0:T(1,128)} %param.16) | copy-start | bytes 1540
  9.6 14.6 %copy-start.15 = (s32[1,1,128]{2,1,0:T(1,128)S(1)}, s32[1,1,128]{2,1,0:T(1,128)}, u32[]{:S(2)}) copy-start(s32[1,1,128]{2,1,0:T(1,128)} %param.15) | copy-start | bytes 1540
  9.7 15.3 %copy-start.4 = (f32[1024,256]{1,0:T(8,128)S(1)}, f32[1024,256]{1,0:T(8,128)}, u32[]{:S(2)}) copy-start(f32[1024,256]{1,0:T(8,128)} %param.10) | copy-start | bytes 3145732
  10.6 35.6 %copy-start.12 = (bf16[1,128,256]{2,1,0:T(8,128)(2,1)S(1)}, bf16[1,128,256]{2,1,0:T(8,128)(2,1)}, u32[]{:S(2)}) copy-start(bf16[1,128,256]{2,1,0:T(8,128)(2,1)} %get-tuple-element.104) | copy-start | bytes 196612
  10.6 40.7 %copy-start.11 = (bf16[1,128,256]{2,1,0:T(8,128)(2,1)S(1)}, bf16[1,128,256]{2,1,0:T(8,128)(2,1)}, u32[]{:S(2)}) copy-start(bf16[1,128,256]{2,1,0:T(8,128)(2,1)} %get-tuple-element.103) | copy-start | bytes 196612
  10.6 46.8 %copy-start.10 = (bf16[1,128,256]{2,1,0:T(8,128)(2,1)S(1)}, bf16[1,128,256]{2,1,0:T(8,128)(2,1)}, u32[]{:S(2)}) copy-start(bf16[1,128,256]{2,1,0:T(8,128)(2,1)} %get-tuple-element.102) | copy-start | bytes 196612
  10.6 52.0 %copy-start.9 = (bf16[1,128,256]{2,1,0:T(8,128)(2,1)S(1)}, bf16[1,128,256]{2,1,0:T(8,128)(2,1)}, u32[]{:S(2)}) copy-start(bf16[1,128,256]{2,1,0:T(8,128)(2,1)} %get-tuple-element.101) | copy-start | bytes 196612
  10.7 71.5 %collective-permute-start.14 = (bf16[1,128,256]{2,1,0:T(8,128)(2,1)S(1)}, bf16[1,128,256]{2,1,0:T(8,128)(2,1)S(1)}, u32[]{:S(2)}, u32[]{:S(2)}) collective-permute-start(bf16[1,128,256]{2,1,0:T(8,128)(2,1)S(1)} %get-tuple-element.95), channel_id=1, source_target_pairs={{0,30},{2,28},{4,26},{6,24},{8,22},{10,20},{12,18},{14,16},{16,14}... | collective-permute-start | bytes 196616 | tf_op jit(solution)/shard_map/ppermute | solution.py:84
  17.7 64.5 %collective-permute-start.13 = (bf16[1,128,256]{2,1,0:T(8,128)(2,1)S(1)}, bf16[1,128,256]{2,1,0:T(8,128)(2,1)S(1)}, u32[]{:S(2)}, u32[]{:S(2)}) collective-permute-start(bf16[1,128,256]{2,1,0:T(8,128)(2,1)S(1)} %get-tuple-element.96), channel_id=1, source_target_pairs={{0,28},{2,30},{4,24},{6,26},{8,20},{10,22},{12,16},{14,18},{16,12}... | collective-permute-start | bytes 196616 | tf_op jit(solution)/shard_map/ppermute | solution.py:84
  17.8 64.3 %collective-permute-start.12 = (bf16[1,128,256]{2,1,0:T(8,128)(2,1)S(1)}, bf16[1,128,256]{2,1,0:T(8,128)(2,1)S(1)}, u32[]{:S(2)}, u32[]{:S(2)}) collective-permute-start(bf16[1,128,256]{2,1,0:T(8,128)(2,1)S(1)} %get-tuple-element.97), channel_id=1, source_target_pairs={{0,26},{2,24},{4,30},{6,28},{8,18},{10,16},{12,22},{14,20},{16,10}... | collective-permute-start | bytes 196616 | tf_op jit(solution)/shard_map/ppermute | solution.py:84
  21.4 60.7 %collective-permute-start.11 = (bf16[1,128,256]{2,1,0:T(8,128)(2,1)S(1)}, bf16[1,128,256]{2,1,0:T(8,128)(2,1)S(1)}, u32[]{:S(2)}, u32[]{:S(2)}) collective-permute-start(bf16[1,128,256]{2,1,0:T(8,128)(2,1)S(1)} %get-tuple-element.98), channel_id=1, source_target_pairs={{0,24},{2,26},{4,28},{6,30},{8,16},{10,18},{12,20},{14,22},{16,8},... | collective-permute-start | bytes 196616 | tf_op jit(solution)/shard_map/ppermute | solution.py:84
  21.6 4.5 %collective-permute-start = (bf16[1,128,256]{2,1,0:T(8,128)(2,1)}, bf16[1,128,256]{2,1,0:T(8,128)(2,1)S(1)}, u32[]{:S(2)}, u32[]{:S(2)}) collective-permute-start(bf16[1,128,256]{2,1,0:T(8,128)(2,1)} %get-tuple-element.109), channel_id=1, source_target_pairs={{0,2},{2,0},{4,6},{6,4},{8,10},{10,8},{12,14},{14,12},{16,18},{18,... | collective-permute-start | bytes 196616 | tf_op jit(solution)/shard_map/ppermute | solution.py:84
  26.1 4.5 %collective-permute-start.1 = (bf16[1,128,256]{2,1,0:T(8,128)(2,1)}, bf16[1,128,256]{2,1,0:T(8,128)(2,1)S(1)}, u32[]{:S(2)}, u32[]{:S(2)}) collective-permute-start(bf16[1,128,256]{2,1,0:T(8,128)(2,1)} %get-tuple-element.108), channel_id=1, source_target_pairs={{0,4},{2,6},{4,0},{6,2},{8,12},{10,14},{12,8},{14,10},{16,20},{18,... | collective-permute-start | bytes 196616 | tf_op jit(solution)/shard_map/ppermute | solution.py:84
  30.5 5.4 %collective-permute-start.2 = (bf16[1,128,256]{2,1,0:T(8,128)(2,1)}, bf16[1,128,256]{2,1,0:T(8,128)(2,1)S(1)}, u32[]{:S(2)}, u32[]{:S(2)}) collective-permute-start(bf16[1,128,256]{2,1,0:T(8,128)(2,1)} %get-tuple-element.107), channel_id=1, source_target_pairs={{0,6},{2,4},{4,2},{6,0},{8,14},{10,12},{12,10},{14,8},{16,22},{18,... | collective-permute-start | bytes 196616 | tf_op jit(solution)/shard_map/ppermute | solution.py:84
  35.9 4.9 %collective-permute-start.3 = (bf16[1,128,256]{2,1,0:T(8,128)(2,1)}, bf16[1,128,256]{2,1,0:T(8,128)(2,1)S(1)}, u32[]{:S(2)}, u32[]{:S(2)}) collective-permute-start(bf16[1,128,256]{2,1,0:T(8,128)(2,1)} %get-tuple-element.106), channel_id=1, source_target_pairs={{0,8},{2,10},{4,12},{6,14},{8,0},{10,2},{12,4},{14,6},{16,24},{18,... | collective-permute-start | bytes 196616 | tf_op jit(solution)/shard_map/ppermute | solution.py:84
  40.8 5.4 %collective-permute-start.4 = (bf16[1,128,256]{2,1,0:T(8,128)(2,1)}, bf16[1,128,256]{2,1,0:T(8,128)(2,1)S(1)}, u32[]{:S(2)}, u32[]{:S(2)}) collective-permute-start(bf16[1,128,256]{2,1,0:T(8,128)(2,1)} %get-tuple-element.105), channel_id=1, source_target_pairs={{0,10},{2,8},{4,14},{6,12},{8,2},{10,0},{12,6},{14,4},{16,26},{18,... | collective-permute-start | bytes 196616 | tf_op jit(solution)/shard_map/ppermute | solution.py:84
  46.2 5.2 %collective-permute-start.5 = (bf16[1,128,256]{2,1,0:T(8,128)(2,1)S(1)}, bf16[1,128,256]{2,1,0:T(8,128)(2,1)S(1)}, u32[]{:S(2)}, u32[]{:S(2)}) collective-permute-start(bf16[1,128,256]{2,1,0:T(8,128)(2,1)S(1)} %copy-done.12), channel_id=1, source_target_pairs={{0,12},{2,14},{4,8},{6,10},{8,4},{10,6},{12,0},{14,2},{16,28},{18,... | collective-permute-start | bytes 196616 | tf_op jit(solution)/shard_map/ppermute | solution.py:84
  51.4 6.1 %collective-permute-start.6 = (bf16[1,128,256]{2,1,0:T(8,128)(2,1)S(1)}, bf16[1,128,256]{2,1,0:T(8,128)(2,1)S(1)}, u32[]{:S(2)}, u32[]{:S(2)}) collective-permute-start(bf16[1,128,256]{2,1,0:T(8,128)(2,1)S(1)} %copy-done.11), channel_id=1, source_target_pairs={{0,14},{2,12},{4,10},{6,8},{8,6},{10,4},{12,2},{14,0},{16,30},{18,... | collective-permute-start | bytes 196616 | tf_op jit(solution)/shard_map/ppermute | solution.py:84
  57.4 5.2 %collective-permute-start.7 = (bf16[1,128,256]{2,1,0:T(8,128)(2,1)S(1)}, bf16[1,128,256]{2,1,0:T(8,128)(2,1)S(1)}, u32[]{:S(2)}, u32[]{:S(2)}) collective-permute-start(bf16[1,128,256]{2,1,0:T(8,128)(2,1)S(1)} %copy-done.10), channel_id=1, source_target_pairs={{0,16},{2,18},{4,20},{6,22},{8,24},{10,26},{12,28},{14,30},{16,0},... | collective-permute-start | bytes 196616 | tf_op jit(solution)/shard_map/ppermute | solution.py:84
  62.6 6.1 %collective-permute-start.8 = (bf16[1,128,256]{2,1,0:T(8,128)(2,1)S(1)}, bf16[1,128,256]{2,1,0:T(8,128)(2,1)S(1)}, u32[]{:S(2)}, u32[]{:S(2)}) collective-permute-start(bf16[1,128,256]{2,1,0:T(8,128)(2,1)S(1)} %copy-done.9), channel_id=1, source_target_pairs={{0,18},{2,16},{4,22},{6,20},{8,26},{10,24},{12,30},{14,28},{16,2},... | collective-permute-start | bytes 196616 | tf_op jit(solution)/shard_map/ppermute | solution.py:84
  68.7 6.4 %collective-permute-start.9 = (bf16[1,128,256]{2,1,0:T(8,128)(2,1)S(1)}, bf16[1,128,256]{2,1,0:T(8,128)(2,1)S(1)}, u32[]{:S(2)}, u32[]{:S(2)}) collective-permute-start(bf16[1,128,256]{2,1,0:T(8,128)(2,1)S(1)} %get-tuple-element.100), channel_id=1, source_target_pairs={{0,20},{2,22},{4,16},{6,18},{8,28},{10,30},{12,24},{14,26},{16,4},... | collective-permute-start | bytes 196616 | tf_op jit(solution)/shard_map/ppermute | solution.py:84
  75.1 7.0 %collective-permute-start.10 = (bf16[1,128,256]{2,1,0:T(8,128)(2,1)S(1)}, bf16[1,128,256]{2,1,0:T(8,128)(2,1)S(1)}, u32[]{:S(2)}, u32[]{:S(2)}) collective-permute-start(bf16[1,128,256]{2,1,0:T(8,128)(2,1)S(1)} %get-tuple-element.99), channel_id=1, source_target_pairs={{0,22},{2,20},{4,18},{6,16},{8,30},{10,28},{12,26},{14,24},{16,6},... | collective-permute-start | bytes 196616 | tf_op jit(solution)/shard_map/ppermute | solution.py:84
  82.2 1.0 copy-start.2
  89.8 4.4 %copy-start.1 = (bf16[32,128,256]{2,1,0:T(8,128)(2,1)S(1)}, bf16[32,128,256]{2,1,0:T(8,128)(2,1)}, u32[]{:S(2)}) copy-start(bf16[32,128,256]{2,1,0:T(8,128)(2,1)} %gather_fusion) | copy-start | bytes 6291460 | tf_op jit(solution)/shard_map/while
  93.3 1.0 copy-start.3
  120.8 4.4 %copy-start.1 = (bf16[32,128,256]{2,1,0:T(8,128)(2,1)S(1)}, bf16[32,128,256]{2,1,0:T(8,128)(2,1)}, u32[]{:S(2)}) copy-start(bf16[32,128,256]{2,1,0:T(8,128)(2,1)} %gather_fusion) | copy-start | bytes 6291460 | tf_op jit(solution)/shard_map/while
  124.2 1.0 copy-start.3
  151.8 4.4 %copy-start.1 = (bf16[32,128,256]{2,1,0:T(8,128)(2,1)S(1)}, bf16[32,128,256]{2,1,0:T(8,128)(2,1)}, u32[]{:S(2)}) copy-start(bf16[32,128,256]{2,1,0:T(8,128)(2,1)} %gather_fusion) | copy-start | bytes 6291460 | tf_op jit(solution)/shard_map/while
  155.2 1.0 copy-start.3
  182.8 4.4 %copy-start.1 = (bf16[32,128,256]{2,1,0:T(8,128)(2,1)S(1)}, bf16[32,128,256]{2,1,0:T(8,128)(2,1)}, u32[]{:S(2)}) copy-start(bf16[32,128,256]{2,1,0:T(8,128)(2,1)} %gather_fusion) | copy-start | bytes 6291460 | tf_op jit(solution)/shard_map/while
  186.2 1.0 copy-start.3
  207.4 24.2 %copy-start = (f32[8,128,256]{2,1,0:T(8,128)}, f32[8,128,256]{2,1,0:T(8,128)S(1)}, u32[]{:S(2)}) copy-start(f32[8,128,256]{2,1,0:T(8,128)S(1)} %get-tuple-element.69) | copy-start | bytes 3145732
  207.4 24.2 %copy-start.13 = (s32[1,1,16]{2,1,0:T(1,128)S(1)}, s32[1,1,16]{2,1,0:T(1,128)}, u32[]{:S(2)}) copy-start(s32[1,1,16]{2,1,0:T(1,128)} %param.17) | copy-start | bytes 196
  231.6 19.9 %copy-start.7 = (f32[256,256]{1,0:T(8,128)S(1)}, f32[256,256]{1,0:T(8,128)}, u32[]{:S(2)}) copy-start(f32[256,256]{1,0:T(8,128)} %param.12) | copy-start | bytes 786436
  231.6 19.9 %copy-start.8 = (f32[256,256]{1,0:T(8,128)S(1)}, f32[256,256]{1,0:T(8,128)}, u32[]{:S(2)}) copy-start(f32[256,256]{1,0:T(8,128)} %param.13) | copy-start | bytes 786436
  231.6 21.7 %copy-start.5 = (f32[1024,256]{1,0:T(8,128)S(1)}, f32[1024,256]{1,0:T(8,128)}, u32[]{:S(2)}) copy-start(f32[1024,256]{1,0:T(8,128)} %param.10) | copy-start | bytes 3145732
  231.6 21.6 %copy-start.6 = (f32[1024,256]{1,0:T(8,128)S(1)}, f32[1024,256]{1,0:T(8,128)}, u32[]{:S(2)}) copy-start(f32[1024,256]{1,0:T(8,128)} %param.11) | copy-start | bytes 3145732
Sparse Core Ops, SparseCore 0:
  233.2 18.2 all-reduce.2
